TPU v7x, 32 devices: a whole 2x2x4 slice. The times are simulated.
32 devices in a mesh: parts: 2 (over y), tm: 8 (over z, x), band: 2 (over core).
Axes of the slice: x: 2, y: 2, z: 4, core: 2. Of those that a mesh axis runs over, the one named last changes fastest.
Arguments:
- query_tokens: bfloat16 [16, 8, 32, 2240], P(('parts', 'tm'), 'band'), parts along dimension 0, may hold values from -6 to 6
- key_tokens: bfloat16 [16, 8, 32, 2240], P(('parts', 'tm'), 'band'), parts along dimension 0, may hold values from -6 to 6
- value_tokens: bfloat16 [16, 8, 32, 2240], P(('parts', 'tm'), 'band'), parts along dimension 0, may hold values from -14 to 14
- norm_gain: float32 [2240], replicated, may hold values from 0.1 to 1.9
- out_weight: bfloat16 [2, 8, 313600], P('band', 'tm'), may hold values from -0.125 to 0.125
Outputs:
- block_out: bfloat16 [16, 8, 32, 2240], P(('parts', 'tm'), 'band'), parts along dimension 0
There are 2 independent parts, one for each index of `parts`. A program takes and returns all parts, laid end to end along the dimension named above; an argument that names none is the same for every part. Nothing has to cross between parts.
All inputs are finite; a program needn't handle non-finite values.
Results may differ from a plain program's by a relative error of at most 0.0049.
Values may be sent and summed in bfloat16 or wider, within the bound.
No kernel may reach another device: no remote copies, remote signals or barrier semaphores. Data moves between devices by JAX's collectives and lax.ppermute only.
A program may use at most 128 MiB of HBM per device.

v0:
```python
import jax
import jax.numpy as jnp
from jax import lax
from jax.sharding import PartitionSpec as P

HEADS = 70
HD = 32
norm_epsilon = 1e-06
read_epsilon = 1e-06


def entering(x, axis, combine, identity):
    peers, place = (lax.axis_size(axis), lax.axis_index(axis))
    everything = jax.tree.map(lambda part: lax.all_gather(part, axis), x)
    start = jax.tree.map(
        lambda part, zero: jnp.broadcast_to(jnp.asarray(zero, part.dtype), part.shape), x, identity
    )

    def hop(k, before):
        reached = k < place
        new = combine(before, jax.tree.map(lambda part: part[k], everything))
        return jax.tree.map(lambda a, b: jnp.where(reached, a, b), new, before)

    return lax.fori_loop(0, peers, hop, start)


def add_pair(earlier, later):
    return (earlier[0] + later[0], earlier[1] + later[1])


def body(query_tokens, key_tokens, value_tokens, norm_gain, out_weight):
    frames, rows, width, depth = query_tokens.shape
    key_relu = jax.nn.relu(key_tokens).reshape(frames, rows * width, HEADS, HD)
    value_heads = value_tokens.reshape(frames, rows * width, HEADS, HD)
    part_state = jnp.einsum(
        "fthd,fthe->fhde", key_relu, value_heads, preferred_element_type=jnp.float32
    ).reshape(frames, HEADS, HD * HD)
    part_norm = jnp.sum(key_relu, axis=1, dtype=jnp.float32)
    state_sum, norm_sum = lax.psum((part_state, part_norm), "band")
    local_state = jnp.cumsum(state_sum, axis=0)
    local_norm = jnp.cumsum(norm_sum, axis=0)
    before = entering(
        (local_state[-1], local_norm[-1]),
        "tm",
        add_pair,
        (jnp.zeros_like(local_state[-1]), jnp.zeros_like(local_norm[-1])),
    )
    prefix_state = local_state + before[0]
    prefix_norm = local_norm + before[1]
    query_relu = jax.nn.relu(query_tokens.astype(jnp.float32)).reshape(
        frames, rows * width, HEADS, HD
    )
    numer = jnp.einsum(
        "fthd,fhde->fthe",
        query_relu,
        prefix_state.reshape(frames, HEADS, HD, HD),
        precision=lax.Precision.HIGHEST,
    )
    denom = (
        jnp.einsum("fthd,fhd->fth", query_relu, prefix_norm, precision=lax.Precision.HIGHEST)
        + read_epsilon
    )
    reads = (numer / denom[:, :, :, None]).reshape(frames * rows * width, depth)
    square = jnp.mean(reads * reads, axis=-1, keepdims=True)
    normed = (reads * lax.rsqrt(square + norm_epsilon) * norm_gain).astype(jnp.bfloat16)
    gathered = lax.all_gather(out_weight, "tm", axis=1, tiled=True)
    rows_half = gathered.reshape(-1, depth)
    result = jnp.dot(
        normed,
        lax.all_gather(rows_half, "band", axis=0, tiled=True),
        preferred_element_type=jnp.float32,
    )
    return result.astype(jnp.bfloat16).reshape(frames, rows, width, depth)


def solution(mesh):
    in_specs = (
        P(("parts", "tm"), "band", None, None),
        P(("parts", "tm"), "band", None, None),
        P(("parts", "tm"), "band", None, None),
        P(),
        P("band", "tm", None),
    )
    out_specs = P(("parts", "tm"), "band", None, None)
    return jax.shard_map(body, mesh=mesh, in_specs=in_specs, out_specs=out_specs, check_vma=False)
```

profile of v0, /device:TPU:0, one launch (start us, length us, event | category | flops | bytes accessed | tf_op | source)
XLA Modules:
  0.0 356.1 jit_solution(12308929848867415624)
XLA Ops:
  7.4 0.0 all-reduce.2.cloned.1.call-start
  7.4 1.1 broadcast_maximum_fusion
  8.5 0.0 copy-start.4
  8.5 2.0 reshape.61
  10.5 0.0 copy-done.4
  10.5 3.0 reshape.62
  13.4 2.4 fusion
  15.9 1.6 copy.32
  17.4 0.0 all-reduce.2.cloned.1.call-update
  17.5 0.0 all-gather.6.cloned.1.call-start
  17.5 0.5 all-gather.6.cloned.1.call-update
  18.0 0.0 all-gather.4.cloned.1.call-start
  18.1 20.8 %all-reduce.2.cloned.1.call-done = f32[1,70,1024]{1,2,0:T(8,128)} async-done(((f32[1,70,1024]{1,2,0:T(8,128)}), f32[1,70,1024]{1,2,0:T(8,128)}) %all-reduce.2.cloned.1.call-update) | async-done | bytes 286736 | tf_op jit(solution)/shard_map/psum | solution.py:39
  38.9 2.0 copy.33
  40.9 0.0 all-gather.4.cloned.1.call-update
  40.9 0.0 all-gather.8.cloned.1.call-start
  41.0 126.2 %all-gather.6.cloned.1.call-done = bf16[1,8,313600]{2,0,1:T(2,128)(2,1)} async-done(((bf16[1,1,313600]{2,0,1:T(2,128)(2,1)}), bf16[1,8,313600]{2,0,1:T(2,128)(2,1)}) %all-gather.6.cloned.1.call-update) | async-done | bytes 5017616 | tf_op jit(solution)/shard_map/all_gather | solution.py:66
  167.2 90.6 %reduce.3 = bf16[8,313600]{1,0:T(8,128)(2,1)} reduce(bf16[1,8,313600]{2,0,1:T(2,128)(2,1)} %all-gather.6.cloned.1.call-done, bf16[]{:T(256)} %constant.55), dimensions={0}, to_apply=%all_gather.14.reduce_sub_computation | reduce | bytes 10035202 | tf_op jit(solution)/shard_map/all_gather | solution.py:66
  257.7 12.1 %reshape.73 = bf16[2508800]{0:T(1024)(128)(2,1)} reshape(bf16[8,313600]{1,0:T(8,128)(2,1)} %reduce.3) | data formatting | bytes 10035200
  269.8 9.4 %reshape.68 = bf16[1120,2240]{1,0:T(8,128)(2,1)} reshape(bf16[2508800]{0:T(1024)(128)(2,1)} %reshape.73) | data formatting | bytes 10035200 | tf_op jit(solution)/shard_map/reshape | solution.py:67
  279.3 0.0 copy-start
  279.3 0.0 all-gather.8.cloned.1.call-update
  279.3 0.0 copy-start.3
  279.3 1.0 copy-done
  280.3 0.1 convert_reduce_fusion
  280.5 0.1 reduce_sum.21
  280.6 3.5 psum.15
  284.0 0.1 copy.34
  284.1 0.0 copy-done.3
  284.1 0.1 convert_maximum_fusion
  284.2 3.7 %reshape.65 = f32[128,70,32]{2,1,0:T(8,128)} reshape(f32[1,4,32,2240]{3,2,1,0:T(8,128)S(1)} %convert_maximum_fusion) | data formatting | bytes 2293760 | tf_op jit(solution)/shard_map/reshape.5
  287.9 4.7 %copy.38 = f32[128,70,32]{0,2,1:T(8,128)S(1)} copy(f32[128,70,32]{2,1,0:T(8,128)} %reshape.65) | data formatting | bytes 2293760 | tf_op jit(solution)/shard_map/reshape.5
  292.6 30.5 %all_gather.13 = f32[8,70,32]{1,2,0:T(8,128)S(1)} all-gather(f32[1,70,32]{1,2,0:T(8,128)S(1)} %copy.34), channel_id=1, replica_groups=mesh['parts'=2,'tm'=8,'band'=2] {'tm'}, dimensions={0}, use_global_device_ids=true | all-gather | bytes 80640 | tf_op jit(solution)/shard_map/all_gather | solution.py:14
  323.1 0.0 all-gather.4.cloned.1.call-done
  323.1 10.0 %while.16 = (s32[]{:T(128)}, f32[70,1024]{1,0:T(8,128)S(1)}, f32[70,32]{1,0:T(8,128)S(1)}, s32[]{:T(128)}, f32[8,70,1024]{2,1,0:T(8,128)}, /*index=5*/f32[8,70,32]{1,2,0:T(8,128)S(1)}, s32[]{:T(128)}, s32[]{:T(128)}) while((s32[]{:T(128)}, f32[70,1024]{1,0:T(8,128)S(1)}, f32[70,32]{1,0:T(8,128)S(1)}, s32[]{:T(128)}, ...), condition=%wide.region_4.5_spmd.clone, body=%wide.region_3.4_spmd.clone.sunk | while | flops 221764 | bytes 922995 | solution.py:24
  323.3 1.1 add_select_fusion.4
  324.4 0.1 copy.52
  324.5 1.1 add_select_fusion.4
  325.6 0.1 copy.52
  325.8 1.1 add_select_fusion.4
  326.9 0.1 copy.52
  327.0 1.1 add_select_fusion.4
  328.1 0.1 copy.52
  328.2 1.1 add_select_fusion.4
  329.3 0.1 copy.52
  329.4 1.1 add_select_fusion.4
  330.5 0.1 copy.52
  330.6 1.1 add_select_fusion.4
  331.7 0.1 copy.52
  331.9 1.1 add_select_fusion.4
  333.0 0.1 copy.52
  333.1 0.0 copy-start.1
  333.1 0.2 copy.36
  333.3 0.8 copy-done.1
  334.1 0.1 bitcast_add_fusion
  334.2 2.0 copy.37
  336.2 1.0 fusion.8
  337.2 0.2 copy-done.2
  337.4 1.5 multiply_reduce_fusion
  338.9 0.0 copy-done.5
  338.9 0.4 fusion.4
  339.3 0.0 all-gather.8.cloned.1.call-done
  339.3 8.1 %convolution_convert_fusion = bf16[128,2240]{0,1:T(8,128)(2,1)S(1)} fusion(bf16[128,2240]{0,1:T(8,128)(2,1)S(1)} %fusion.4, bf16[2240,2240]{1,0:T(8,128)(2,1)} %all-gather.8.cloned.1.call-done), kind=kOutput, calls=%fused_computation.3 | convolution fusion | flops 1284792320 | bytes 11182080 | tf_op jit(solution)/shard_map/dot_general | solution.py:68
  347.4 1.1 copy.40
  (23 shorter events, 0.2 us)
Async XLA Ops:
  7.4 31.6 %all-reduce.2.cloned.1.call-start = ((), (), s32[]{:S(2)}) async-start(), calls=%async_computation | async-start | bytes 1048576 | tf_op jit(solution)/shard_map/psum | solution.py:39
  8.5 2.0 copy-start.4
  17.5 149.7 %all-gather.6.cloned.1.call-start = ((), (), s32[]{:S(2)}) async-start(), calls=%async_computation.2 | async-start | bytes 11289600 | tf_op jit(solution)/shard_map/all_gather | solution.py:66
  18.0 305.1 %all-gather.4.cloned.1.call-start = ((), (), s32[]{:S(2)}) async-start(), calls=%async_computation.1 | async-start | bytes 2654208 | tf_op jit(solution)/shard_map/all_gather | solution.py:14
  40.9 298.4 %all-gather.8.cloned.1.call-start = ((), (), s32[]{:S(2)}) async-start(), calls=%async_computation.3 | async-start | bytes 15482880 | tf_op jit(solution)/shard_map/all_gather | solution.py:70
  279.3 1.1 copy-start
  279.3 4.8 %copy-start.3 = (bf16[1,4,32,2240]{3,2,1,0:T(8,128)(2,1)S(1)}, bf16[1,4,32,2240]{3,2,1,0:T(8,128)(2,1)}, u32[]{:S(2)}) copy-start(bf16[1,4,32,2240]{3,2,1,0:T(8,128)(2,1)} %param.7) | copy-start | bytes 1720324
  333.1 1.0 copy-start.1
  336.1 1.3 copy-start.2
  337.4 1.5 copy-start.5
Sparse Core Ops, SparseCore 0:
  17.6 21.3 all-reduce.1
Sparse Core Ops, SparseCore 1:
  20.1 147.0 all-gather.5
  169.2 49.8 all-gather.3
  279.4 20.5 all-gather.7
where the time goes:
time: 357 us; the launch traced here: 356 us
  waiting for transfers between devices  148 us (41%)
  other arithmetic  101 us (28%)
  local copies, waits for them, and re-layouts  44.7 us (13%)
  blocking collectives  34 us (10%)
  between operations  15.2 us (4%)
  matrix products  13 us (4%)
    all_gather x1, waiting for transfers between devices, body(): gathered = lax.all_gather(out_weight, 'tm', axis=1, tiled=True)  126 us
    all_gather x1, other arithmetic, body(): gathered = lax.all_gather(out_weight, 'tm', axis=1, tiled=True)  90.6 us
    all_gather x1, blocking collectives, entering(): everything = jax.tree.map(lambda part: lax.all_gather(part, axis), x)  30.5 us
    psum x1, waiting for transfers between devices, body(): state_sum, norm_sum = lax.psum((part_state, part_norm), 'band')  20.8 us
    unnamed x13, local copies, waits for them, and re-layouts  14.1 us
    another operation x4, local copies, waits for them, and re-layouts  13.3 us
    reshape x1, local copies, waits for them, and re-layouts, body(): rows_half = gathered.reshape(-1, depth)  9.45 us
    select_n x16, other arithmetic, hop(): return jax.tree.map(lambda a, b: jnp.where(reached, a, b), new, before)  8.63 us
  transfers between devices with their start and end apart: 4, of which 2 were waited for; matrix products, arithmetic and copies ran while one was open for 39% of the time, Pallas kernels for 0%

commit v1 on v0

--- a/solution.py
+++ b/solution.py
@@ -63,7 +63,12 @@
     reads = (numer / denom[:, :, :, None]).reshape(frames * rows * width, depth)
     square = jnp.mean(reads * reads, axis=-1, keepdims=True)
     normed = (reads * lax.rsqrt(square + norm_epsilon) * norm_gain).astype(jnp.bfloat16)
-    gathered = lax.all_gather(out_weight, "tm", axis=1, tiled=True)
+    ring = [out_weight]
+    for hop_ in range(7):
+        ring.append(lax.ppermute(ring[-1], "tm", [(dev, (dev + 1) % 8) for dev in range(8)]))
+    gathered = jnp.roll(
+        jnp.concatenate(ring[::-1], axis=1), (lax.axis_index("tm") + 1) * ring[0].shape[1], axis=1
+    )
     rows_half = gathered.reshape(-1, depth)
     result = jnp.dot(
         normed,

time: 357 us -> 385 us (1.078); the launches traced: 356 us -> 378 us
  other arithmetic: 101 us -> 10.5 us
  local copies, waits for them, and re-layouts: 44.7 us -> 109 us
  waiting for transfers between devices: 148 us -> 193 us
    ppermute x0 -> x7, waiting for transfers between devices: none -> 174 us  [body(): lax.ppermute(ring[-1], 'tm', [(dev, (dev + 1) % 8) for dev in range(8)])]
    all_gather x1 -> x0, waiting for transfers between devices: 126 us -> none  [body(): gathered = lax.all_gather(out_weight, 'tm', axis=1, tiled=True)]
    all_gather x1 -> x0, other arithmetic: 90.6 us -> none  [body(): gathered = lax.all_gather(out_weight, 'tm', axis=1, tiled=True)]
    concatenate x0 -> x1, local copies, waits for them, and re-layouts: none -> 52.3 us  [body(): jnp.roll(jnp.concatenate(ring[::-1], axis=1), (lax.axis_index('tm') + 1)...]
    dynamic_slice x0 -> x1, local copies, waits for them, and re-layouts: none -> 7.4 us  [body(): jnp.roll(jnp.concatenate(ring[::-1], axis=1), (lax.axis_index('tm') + 1)...]
    unnamed x13 -> x25, local copies, waits for them, and re-layouts: 14.1 us -> 17.6 us
  transfers between devices with their start and end apart: 4 -> 10, of which waited for: 2 -> 7; matrix products, arithmetic and copies ran while one was open for 39% -> 31% of each run, Pallas kernels for 0% -> 0%
where the time goes in v1:
time: 385 us; the launch traced here: 378 us
  waiting for transfers between devices  193 us (50%)
  local copies, waits for them, and re-layouts  109 us (28%)
  blocking collectives  34.6 us (9%)
  matrix products  14.1 us (4%)
  between operations  13.3 us (3%)
  other arithmetic  10.5 us (3%)
    ppermute x7, waiting for transfers between devices, body(): lax.ppermute(ring[-1], 'tm', [(dev, (dev + 1) % 8) for dev in range(8)])  174 us
    concatenate x1, local copies, waits for them, and re-layouts, body(): jnp.roll(jnp.concatenate(ring[::-1], axis=1), (lax.axis_index('tm') + 1)...  52.3 us
    all_gather x1, blocking collectives, entering(): everything = jax.tree.map(lambda part: lax.all_gather(part, axis), x)  30.9 us
    psum x1, waiting for transfers between devices, body(): state_sum, norm_sum = lax.psum((part_state, part_norm), 'band')  19.2 us
    unnamed x25, local copies, waits for them, and re-layouts  17.6 us
    another operation x4, local copies, waits for them, and re-layouts  13.1 us
    reshape x1, local copies, waits for them, and re-layouts, body(): rows_half = gathered.reshape(-1, depth)  9.45 us
    select_n x16, other arithmetic, hop(): return jax.tree.map(lambda a, b: jnp.where(reached, a, b), new, before)  8.68 us
  transfers between devices with their start and end apart: 10, of which 7 were waited for; matrix products, arithmetic and copies ran while one was open for 31% of the time, Pallas kernels for 0%

profile of v1, /device:TPU:0, one launch (start us, length us, event | category | flops | bytes accessed | tf_op | source)
XLA Modules:
  0.0 377.9 jit_solution(11964030976587311869)
XLA Ops:
  6.5 3.0 collective-permute-start
  9.5 30.8 %collective-permute-done = bf16[1,1,313600]{2,1,0:T(2,128)(2,1)S(1)} collective-permute-done((bf16[1,1,313600]{2,1,0:T(2,128)(2,1)}, bf16[1,1,313600]{2,1,0:T(2,128)(2,1)S(1)}, u32[]{:S(2)}, u32[]{:S(2)}) %collective-permute-start) | collective-permute-done | bytes 627232 | tf_op jit(solution)/shard_map/ppermute | solution.py:68
  40.3 1.1 copy-done.1
  41.4 31.4 %collective-permute-done.1 = bf16[1,1,313600]{2,1,0:T(2,128)(2,1)S(1)} collective-permute-done((bf16[1,1,313600]{2,1,0:T(2,128)(2,1)S(1)}, bf16[1,1,313600]{2,1,0:T(2,128)(2,1)S(1)}, u32[]{:S(2)}, u32[]{:S(2)}) %collective-permute-start.1) | collective-permute-done | bytes 627232 | tf_op jit(solution)/shard_map/ppermute | solution.py:68
  72.8 1.1 copy-done.3
  73.9 30.6 %collective-permute-done.2 = bf16[1,1,313600]{2,1,0:T(2,128)(2,1)S(1)} collective-permute-done((bf16[1,1,313600]{2,1,0:T(2,128)(2,1)S(1)}, bf16[1,1,313600]{2,1,0:T(2,128)(2,1)S(1)}, u32[]{:S(2)}, u32[]{:S(2)}) %collective-permute-start.2) | collective-permute-done | bytes 627232 | tf_op jit(solution)/shard_map/ppermute | solution.py:68
  104.5 1.0 copy-done.4
  105.5 29.7 %collective-permute-done.3 = bf16[1,1,313600]{2,1,0:T(2,128)(2,1)S(1)} collective-permute-done((bf16[1,1,313600]{2,1,0:T(2,128)(2,1)S(1)}, bf16[1,1,313600]{2,1,0:T(2,128)(2,1)S(1)}, u32[]{:S(2)}, u32[]{:S(2)}) %collective-permute-start.3) | collective-permute-done | bytes 627232 | tf_op jit(solution)/shard_map/ppermute | solution.py:68
  135.2 1.1 copy-done.5
  136.3 29.0 %collective-permute-done.4 = bf16[1,1,313600]{2,1,0:T(2,128)(2,1)} collective-permute-done((bf16[1,1,313600]{2,1,0:T(2,128)(2,1)S(1)}, bf16[1,1,313600]{2,1,0:T(2,128)(2,1)}, u32[]{:S(2)}, u32[]{:S(2)}) %collective-permute-start.4) | collective-permute-done | bytes 627232 | tf_op jit(solution)/shard_map/ppermute | solution.py:68
  165.3 1.1 broadcast_maximum_fusion
  166.4 0.0 copy-start.10
  166.4 2.0 reshape.61
  168.4 3.0 reshape.62
  171.4 22.3 %collective-permute-done.5 = bf16[1,1,313600]{2,1,0:T(2,128)(2,1)} collective-permute-done((bf16[1,1,313600]{2,1,0:T(2,128)(2,1)}, bf16[1,1,313600]{2,1,0:T(2,128)(2,1)}, u32[]{:S(2)}, u32[]{:S(2)}) %collective-permute-start.5) | collective-permute-done | bytes 627232 | tf_op jit(solution)/shard_map/ppermute | solution.py:68
  193.6 3.4 fusion
  197.1 2.8 copy.21
  199.9 0.0 all-reduce.2.cloned.1.call-update
  199.9 0.0 all-gather.3.cloned.1.call-start
  200.0 19.2 %all-reduce.2.cloned.1.call-done = f32[1,70,1024]{1,2,0:T(8,128)} async-done(((f32[1,70,1024]{1,2,0:T(8,128)}), f32[1,70,1024]{1,2,0:T(8,128)}) %all-reduce.2.cloned.1.call-update) | async-done | bytes 286736 | tf_op jit(solution)/shard_map/psum | solution.py:39
  219.1 2.0 copy.22
  221.1 0.0 all-gather.3.cloned.1.call-update
  221.1 0.2 all-gather.5.cloned.1.call-start
  221.4 52.3 %concatenate.6 = bf16[1,16,313600]{2,1,0:T(8,128)(2,1)} concatenate(bf16[1,1,313600]{2,1,0:T(2,128)(2,1)} %collective-permute-done.6, bf16[1,1,313600]{2,1,0:T(2,128)(2,1)} %collective-permute-done.5, bf16[1,1,313600]{2,1,0:T(2,128)(2,1)} %collective-permute-done.4, bf16[1,1,313600]{2,1,0:T(2,128)(2,1)} %copy-done.5, bf16[1,1,313600]{2,1,0:T(2,128)(2,1)} %copy-done.4, ...), dimensions={1} | concatenate | bytes 20070400 | tf_op jit(solution)/shard_map/jit(_roll_dynamic)/concatenate | solution.py:69
  273.7 7.4 %constant_dynamic-slice_fusion.1 = bf16[1,8,313600]{2,1,0:T(8,128)(2,1)} fusion(bf16[1,16,313600]{2,1,0:T(8,128)(2,1)} %concatenate.6, s32[]{:T(128)S(6)} %select_n.52), kind=kLoop, calls=%fused_computation.24 | loop fusion | bytes 10035204 | tf_op jit(solution)/shard_map/jit(_roll_dynamic)/dynamic_slice | solution.py:69
  281.1 12.1 %reshape.72 = bf16[2508800]{0:T(1024)(128)(2,1)} reshape(bf16[1,8,313600]{2,1,0:T(8,128)(2,1)} %constant_dynamic-slice_fusion.1) | data formatting | bytes 10035200
  293.2 9.4 %reshape.68 = bf16[1120,2240]{1,0:T(8,128)(2,1)} reshape(bf16[2508800]{0:T(1024)(128)(2,1)} %reshape.72) | data formatting | bytes 10035200 | tf_op jit(solution)/shard_map/reshape | solution.py:72
  302.6 0.0 all-gather.5.cloned.1.call-update
  302.7 1.0 copy-done.6
  303.7 0.1 convert_reduce_fusion
  303.8 0.1 reduce_sum.21
  303.9 3.8 psum.15
  307.7 0.1 copy.23
  307.7 0.1 convert_maximum_fusion
  307.8 3.4 reshape.65
  311.2 4.9 %copy.27 = f32[128,70,32]{0,2,1:T(8,128)S(1)} copy(f32[128,70,32]{2,1,0:T(8,128)} %reshape.65) | data formatting | bytes 2293760 | tf_op jit(solution)/shard_map/reshape.5
  316.1 30.9 %all_gather.10 = f32[8,70,32]{1,2,0:T(8,128)S(1)} all-gather(f32[1,70,32]{1,2,0:T(8,128)S(1)} %copy.23), channel_id=1, replica_groups=mesh['parts'=2,'tm'=8,'band'=2] {'tm'}, dimensions={0}, use_global_device_ids=true | all-gather | bytes 80640 | tf_op jit(solution)/shard_map/all_gather | solution.py:14
  347.0 9.8 %while.16 = (s32[]{:T(128)}, f32[70,1024]{1,0:T(8,128)S(1)}, f32[70,32]{1,0:T(8,128)S(1)}, s32[]{:T(128)}, f32[8,70,1024]{2,1,0:T(8,128)}, /*index=5*/f32[8,70,32]{1,2,0:T(8,128)S(1)}, s32[]{:T(128)}, s32[]{:T(128)}) while((s32[]{:T(128)}, f32[70,1024]{1,0:T(8,128)S(1)}, f32[70,32]{1,0:T(8,128)S(1)}, s32[]{:T(128)}, ...), condition=%wide.region_4.5_spmd.clone, body=%wide.region_3.4_spmd.clone.sunk | while | flops 221764 | bytes 922995 | solution.py:24
  347.0 1.1 add_select_fusion.4
  348.1 0.1 copy.40
  348.3 1.1 add_select_fusion.4
  349.4 0.1 copy.40
  349.5 1.1 add_select_fusion.4
  350.6 0.1 copy.40
  350.7 1.1 add_select_fusion.4
  351.8 0.1 copy.40
  351.9 1.1 add_select_fusion.4
  353.0 0.1 copy.40
  353.2 1.1 add_select_fusion.4
  354.2 0.1 copy.40
  354.4 1.1 add_select_fusion.4
  355.5 0.1 copy.40
  355.6 1.1 add_select_fusion.4
  356.7 0.1 copy.40
  356.8 0.2 copy.25
  357.0 0.1 bitcast_add_fusion
  357.1 1.9 copy.26
  359.0 1.0 fusion.8
  360.1 0.2 copy-done.8
  360.3 1.5 multiply_reduce_fusion
  361.8 0.4 fusion.4
  362.1 0.0 all-gather.5.cloned.1.call-done
  362.2 8.1 %convolution_convert_fusion = bf16[128,2240]{0,1:T(8,128)(2,1)S(1)} fusion(bf16[128,2240]{0,1:T(8,128)(2,1)S(1)} %fusion.4, bf16[2240,2240]{1,0:T(8,128)(2,1)} %all-gather.5.cloned.1.call-done), kind=kOutput, calls=%fused_computation.3 | convolution fusion | flops 1284792320 | bytes 11182080 | tf_op jit(solution)/shard_map/dot_general | solution.py:73
  370.3 1.1 copy.28
  (47 shorter events, 0.2 us)
Async XLA Ops:
  6.5 212.6 %all-reduce.2.cloned.1.call-start = ((), (), s32[]{:S(2)}) async-start(), calls=%async_computation | async-start | bytes 1048576 | tf_op jit(solution)/shard_map/psum | solution.py:39
  6.5 33.8 %collective-permute-start = (bf16[1,1,313600]{2,1,0:T(2,128)(2,1)}, bf16[1,1,313600]{2,1,0:T(2,128)(2,1)S(1)}, u32[]{:S(2)}, u32[]{:S(2)}) collective-permute-start(bf16[1,1,313600]{2,1,0:T(2,128)(2,1)} %param.11), channel_id=1, source_target_pairs={{0,2},{2,4},{4,6},{6,8},{8,10},{10,12},{12,14},{14,0},{1,3},{3,5},... | collective-permute-start | bytes 1881608 | tf_op jit(solution)/shard_map/ppermute | solution.py:68
  40.3 1.1 copy-start.1
  41.4 31.4 %collective-permute-start.1 = (bf16[1,1,313600]{2,1,0:T(2,128)(2,1)S(1)}, bf16[1,1,313600]{2,1,0:T(2,128)(2,1)S(1)}, u32[]{:S(2)}, u32[]{:S(2)}) collective-permute-start(bf16[1,1,313600]{2,1,0:T(2,128)(2,1)S(1)} %collective-permute-done), channel_id=1, source_target_pairs={{0,2},{2,4},{4,6},{6,8},{8,10},{10,12},{12,14},{14,0},{1,3},{3,5},... | collective-permute-start | bytes 1881608 | tf_op jit(solution)/shard_map/ppermute | solution.py:68
  72.8 1.1 copy-start.3
  73.9 30.6 %collective-permute-start.2 = (bf16[1,1,313600]{2,1,0:T(2,128)(2,1)S(1)}, bf16[1,1,313600]{2,1,0:T(2,128)(2,1)S(1)}, u32[]{:S(2)}, u32[]{:S(2)}) collective-permute-start(bf16[1,1,313600]{2,1,0:T(2,128)(2,1)S(1)} %collective-permute-done.1), channel_id=1, source_target_pairs={{0,2},{2,4},{4,6},{6,8},{8,10},{10,12},{12,14},{14,0},{1,3},{3,5},... | collective-permute-start | bytes 1881608 | tf_op jit(solution)/shard_map/ppermute | solution.py:68
  104.5 1.1 copy-start.4
  105.5 29.7 %collective-permute-start.3 = (bf16[1,1,313600]{2,1,0:T(2,128)(2,1)S(1)}, bf16[1,1,313600]{2,1,0:T(2,128)(2,1)S(1)}, u32[]{:S(2)}, u32[]{:S(2)}) collective-permute-start(bf16[1,1,313600]{2,1,0:T(2,128)(2,1)S(1)} %collective-permute-done.2), channel_id=1, source_target_pairs={{0,2},{2,4},{4,6},{6,8},{8,10},{10,12},{12,14},{14,0},{1,3},{3,5},... | collective-permute-start | bytes 1881608 | tf_op jit(solution)/shard_map/ppermute | solution.py:68
  135.2 1.1 copy-start.5
  136.3 29.0 %collective-permute-start.4 = (bf16[1,1,313600]{2,1,0:T(2,128)(2,1)S(1)}, bf16[1,1,313600]{2,1,0:T(2,128)(2,1)}, u32[]{:S(2)}, u32[]{:S(2)}) collective-permute-start(bf16[1,1,313600]{2,1,0:T(2,128)(2,1)S(1)} %collective-permute-done.3), channel_id=1, source_target_pairs={{0,2},{2,4},{4,6},{6,8},{8,10},{10,12},{12,14},{14,0},{1,3},{3,5},... | collective-permute-start | bytes 1881608 | tf_op jit(solution)/shard_map/ppermute | solution.py:68
  165.3 28.3 %collective-permute-start.5 = (bf16[1,1,313600]{2,1,0:T(2,128)(2,1)}, bf16[1,1,313600]{2,1,0:T(2,128)(2,1)}, u32[]{:S(2)}, u32[]{:S(2)}) collective-permute-start(bf16[1,1,313600]{2,1,0:T(2,128)(2,1)} %collective-permute-done.4), channel_id=1, source_target_pairs={{0,2},{2,4},{4,6},{6,8},{8,10},{10,12},{12,14},{14,0},{1,3},{3,5},... | collective-permute-start | bytes 1881608 | tf_op jit(solution)/shard_map/ppermute | solution.py:68
  166.4 2.0 copy-start.10
  193.6 27.7 %collective-permute-start.6 = (bf16[1,1,313600]{2,1,0:T(2,128)(2,1)}, bf16[1,1,313600]{2,1,0:T(2,128)(2,1)}, u32[]{:S(2)}, u32[]{:S(2)}) collective-permute-start(bf16[1,1,313600]{2,1,0:T(2,128)(2,1)} %collective-permute-done.5), channel_id=1, source_target_pairs={{0,2},{2,4},{4,6},{6,8},{8,10},{10,12},{12,14},{14,0},{1,3},{3,5},... | collective-permute-start | bytes 1881608 | tf_op jit(solution)/shard_map/ppermute | solution.py:68
  197.1 24.3 %copy-start.2 = (bf16[1,1,313600]{2,1,0:T(2,128)(2,1)S(1)}, bf16[1,1,313600]{2,1,0:T(2,128)(2,1)}, u32[]{:S(2)}) copy-start(bf16[1,1,313600]{2,1,0:T(2,128)(2,1)} %copy-done.1) | copy-start | bytes 1881604
  199.9 21.5 %copy-start = (bf16[1,1,313600]{2,1,0:T(2,128)(2,1)S(1)}, bf16[1,1,313600]{2,1,0:T(2,128)(2,1)}, u32[]{:S(2)}) copy-start(bf16[1,1,313600]{2,1,0:T(2,128)(2,1)} %param.11) | copy-start | bytes 1881604
  199.9 147.1 %all-gather.3.cloned.1.call-start = ((), (), s32[]{:S(2)}) async-start(), calls=%async_computation.1 | async-start | bytes 2654208 | tf_op jit(solution)/shard_map/all_gather | solution.py:14
  221.1 141.0 %all-gather.5.cloned.1.call-start = ((), (), s32[]{:S(2)}) async-start(), calls=%async_computation.2 | async-start | bytes 15482880 | tf_op jit(solution)/shard_map/all_gather | solution.py:75
  302.6 1.1 copy-start.6
  302.6 5.1 %copy-start.9 = (bf16[1,4,32,2240]{3,2,1,0:T(8,128)(2,1)S(1)}, bf16[1,4,32,2240]{3,2,1,0:T(8,128)(2,1)}, u32[]{:S(2)}) copy-start(bf16[1,4,32,2240]{3,2,1,0:T(8,128)(2,1)} %param.7) | copy-start | bytes 1720324
  347.0 10.0 %copy-start.7 = (f32[1,70,1024]{1,2,0:T(8,128)S(1)}, f32[1,70,1024]{1,2,0:T(8,128)}, u32[]{:S(2)}) copy-start(f32[1,70,1024]{1,2,0:T(8,128)} %all-reduce.2.cloned.1.call-done) | copy-start | bytes 860164
  359.0 1.3 copy-start.8
  360.3 1.5 copy-start.11
Sparse Core Ops, SparseCore 0:
  200.0 19.0 all-reduce.1
  221.3 53.0 all-gather.2
  302.8 22.7 all-gather.4
